TPU v7x, 32 devices: a whole 2x2x4 slice. The times are simulated.
32 devices in a mesh: ctx: 4 (over y, core), head: 2 (over x), batch: 4 (over z).
Axes of the slice: x: 2, y: 2, z: 4, core: 2. Of those that a mesh axis runs over, the one named last changes fastest.
Arguments:
- ingest: bfloat16 [4, 4, 12, 128, 4, 256], P('ctx', 'batch', None, None, None, 'head'), may hold values from -6 to 6
- src_shard: int32 [4, 4, 6], P('ctx'), may hold values from 0 to 3, as said below
- src_slot: int32 [4, 4, 6], P('ctx'), may hold values from 0 to 11
- hist_len: int32 [4, 4], P('batch'), may hold values from 1 to 1536, 3072 in all within a row
- w_out: bfloat16 [256, 256], P('head'), may hold values from -0.375 to 0.375
Outputs:
- mixed: bfloat16 [4, 3072, 256], P('batch', 'ctx', 'head')
Inputs may be any that keep to these rules, and one draw needn't show every extreme that they name: `src_shard`: for each owner index, every owner's 6 blocks come from exactly two different ingestion shards, 3 from each; no (shard, slot) pair of one owner index feeds two blocks. `hist_len`: the 4 histories of a group fill its 3072 positions in order.
All inputs are finite; a program needn't handle non-finite values.
Results may differ from a plain program's by a relative error of at most 0.0058.
Values may be sent and summed in bfloat16 or wider, within the bound.
A program may use at most 64 MiB of HBM per device.

v0:
```python
import functools
import math

import jax
import jax.numpy as jnp
from jax import lax
from jax.experimental import pallas as pl
from jax.experimental.pallas import tpu as pltpu
from jax.sharding import PartitionSpec as P

HD = 128
MESH = pl.DeviceIdType.MESH
QUERY, KEY, VALUE, UPDATE = 0, 1, 2, 3
FIRST_KINDS = (KEY, VALUE, QUERY)


def partner(me, mask, count):
    out = 0
    bit = 1
    while bit < count:
        out = out + lax.rem(lax.div(me, bit) + (mask // bit) % 2, 2) * bit
        bit *= 2
    return out


def update_chunks(capacity, rows):
    half = rows // 2
    return [(k, 0, rows) for k in range(capacity - 1)] + [(capacity - 1, 0, half), (capacity - 1, half, half)]


def kernel(sizes, shard_hbm, slot_hbm, hist_hbm, ingest_hbm, w_hbm, out_ref,
           shard_ref, slot_ref, hist_ref, w_ref, local_sems,
           ingest_ref,
           send_bufs, send_u, recv_bufs, recv_u, own_k, own_v, own_q, prev_k, prev_v,
           start_ref, att, gated, w_cols, mixed,
           z_send, z_recv, u_send, u_recv, c_send, c_recv, h_send, h_recv, w_send, w_recv,
           ingest_sem, from_low, from_high):
    groups, ctxs, heads, per_owner, rows = sizes
    capacity = per_owner // 2
    chunks = update_chunks(capacity, rows)
    window = ctxs // 2
    row_count = per_owner * rows
    my_group = lax.axis_index("batch")
    my_ctx = lax.axis_index("ctx")
    my_head = lax.axis_index("head")

    barrier = pltpu.get_barrier_semaphore()
    ingest_copy = pltpu.make_async_copy(ingest_hbm, ingest_ref, ingest_sem)
    ingest_copy.start()
    local_copies = [pltpu.make_async_copy(src, dst, local_sems.at[i]) for i, (src, dst) in enumerate((
        (shard_hbm, shard_ref), (slot_hbm, slot_ref), (hist_hbm, hist_ref), (w_hbm, w_ref)))]
    for copy in local_copies:
        copy.start()
    for axis, me, count in (("ctx", my_ctx, ctxs), ("head", my_head, heads)):
        for offset in range(1, count):
            pl.semaphore_signal(barrier, inc=1, device_id={axis: lax.rem(me + offset, count)}, device_id_type=MESH)
    has_low, has_high = my_group > 0, my_group < groups - 1

    def tell(there, semaphore, to):
        @pl.when(there)
        def _():
            pl.semaphore_signal(semaphore, inc=1, device_id={"batch": to}, device_id_type=MESH)

    tell(has_low, barrier, my_group - 1)
    tell(has_high, barrier, my_group + 1)
    neighbours = jnp.where(has_low, 1, 0) + jnp.where(has_high, 1, 0)

    for copy in local_copies:
        copy.wait()
    slots = []
    for dst in range(groups):
        picked = [jnp.int32(0)] * capacity
        seen = jnp.int32(0)
        for j in range(per_owner):
            hit = shard_ref[dst, j] == my_group
            slot = slot_ref[dst, j]
            for k in range(capacity):
                picked[k] = jnp.where(hit & (seen == k), slot, picked[k])
            seen = seen + jnp.where(hit, 1, 0)
        slots.append(picked)

    sources = [shard_ref[my_group, j] for j in range(per_owner)]
    ranks, sides = [], []
    for j in range(per_owner):
        rank = jnp.int32(0)
        for i in range(j):
            rank = rank + jnp.where(sources[i] == sources[j], 1, 0)
        ranks.append(jnp.minimum(rank, capacity - 1))
        sides.append(jnp.where(sources[j] == sources[0], 0, 1))

    def split_kind(kind):
        width = 4 * rows
        row = lax.broadcasted_iota(jnp.int32, (rows, width), 0)
        col = lax.broadcasted_iota(jnp.int32, (rows, width), 1)
        pick = jnp.where(col == row * 4 + kind, 1.0, 0.0).astype(jnp.bfloat16)

        def one(dst, k):
            block = ingest_ref[slots[dst][k]]
            return jnp.dot(pick, block, preferred_element_type=jnp.float32).astype(jnp.bfloat16)

        return one

    masks = list(range(groups - 1, 0, -1))
    peers = {m: partner(my_group, m, groups) for m in masks}

    def fill(kind):
        one = split_kind(kind)
        for dst in range(groups):
            for k in range(capacity):
                if kind == UPDATE:
                    block = one(dst, k)
                    for c, (of, low, size) in enumerate(chunks):
                        if of == k:
                            send_u[c][dst] = block[low:low + size]
                else:
                    send_bufs[FIRST_KINDS.index(kind), dst, k] = one(dst, k)

    copies = {}

    def send(kind):
        if kind == UPDATE:
            for c in range(len(chunks)):
                for m in masks:
                    copies[kind, c, m] = pltpu.make_async_remote_copy(
                        src_ref=send_u[c].at[peers[m]], dst_ref=recv_u[c].at[my_group],
                        send_sem=u_send.at[c, m], recv_sem=u_recv.at[c, m],
                        device_id={"batch": peers[m]}, device_id_type=MESH)
                    copies[kind, c, m].start()
                recv_u[c][my_group] = send_u[c][my_group]
            return
        n = FIRST_KINDS.index(kind)
        for m in masks:
            copies[kind, m] = pltpu.make_async_remote_copy(
                src_ref=send_bufs.at[n, peers[m]], dst_ref=recv_bufs[n].at[my_group],
                send_sem=z_send.at[n, m], recv_sem=z_recv.at[n, m],
                device_id={"batch": peers[m]}, device_id_type=MESH)
            if kind != KEY:
                copies[kind, m].start()
        recv_bufs[n][my_group] = send_bufs[n, my_group]

    def collect(kind, own_ref):
        n = FIRST_KINDS.index(kind)
        for m in masks:
            copies[kind, m].wait()
        for j in range(per_owner):
            own_ref[j * rows:(j + 1) * rows, :] = recv_bufs[n][sources[j], ranks[j]]

    def start_at(distance):
        for m in masks:
            @pl.when((peers[m] - my_group == distance) | (my_group - peers[m] == distance))
            def _():
                copies[KEY, m].start()

    def hear(distance):
        for there, semaphore in ((my_group >= distance, from_low), (my_group + distance < groups, from_high)):
            @pl.when(there)
            def _():
                pl.semaphore_wait(semaphore.at[distance], 1)

    def pass_on(distance):
        tell((my_group >= distance) & has_high, from_low.at[distance + 1], my_group + 1)
        tell((my_group + distance < groups) & has_low, from_high.at[distance + 1], my_group - 1)

    ingest_copy.wait()
    fill(KEY)
    pl.semaphore_wait(barrier, neighbours + ctxs + heads - 2)
    if groups > 2:
        pass_on(1)
    send(KEY)
    start_at(1)
    fill(VALUE)
    for distance in range(2, groups):
        hear(distance)
        if distance + 1 < groups:
            pass_on(distance)
        start_at(distance)
    send(VALUE)
    fill(QUERY)
    send(QUERY)
    fill(UPDATE)
    send(UPDATE)

    w_copies = []
    for offset in range(1, heads):
        to = lax.rem(my_head + offset, heads)
        copy = pltpu.make_async_remote_copy(
            src_ref=w_ref.at[:, pl.ds(pl.multiple_of(to * HD, HD), HD)], dst_ref=w_cols.at[my_head],
            send_sem=w_send.at[offset], recv_sem=w_recv.at[offset],
            device_id={"head": to}, device_id_type=MESH)
        copy.start()
        w_copies.append(copy)
    w_cols[my_head] = w_ref[:, pl.ds(pl.multiple_of(my_head * HD, HD), HD)]

    ends, total = [], jnp.int32(0)
    for u in range(hist_ref.shape[0]):
        total = total + hist_ref[u]
        ends.append(total)
    base = my_ctx * row_count
    position = base + lax.broadcasted_iota(jnp.int32, (row_count, HD), 0)
    first = jnp.zeros((row_count, HD), jnp.int32)
    for end in ends:
        first = jnp.where(position >= end, end, first)
    start_ref[...] = first - base

    def ctx_copy(n, own_ref, prev_ref, offset):
        return pltpu.make_async_remote_copy(
            src_ref=own_ref, dst_ref=prev_ref.at[offset - 1],
            send_sem=c_send.at[n, offset - 1], recv_sem=c_recv.at[n, offset - 1],
            device_id={"ctx": lax.rem(my_ctx + offset, ctxs)}, device_id_type=MESH)

    def push(n, own_ref, prev_ref):
        for offset in range(1, window + 1):
            @pl.when(my_ctx + offset < ctxs)
            def _():
                ctx_copy(n, own_ref, prev_ref, offset).start()

    collect(KEY, own_k)
    push(0, own_k, prev_k)
    collect(VALUE, own_v)
    push(1, own_v, prev_v)
    collect(QUERY, own_q)

    tile = 2 * rows if per_owner % 2 == 0 else rows
    tiles = row_count // tile
    half_scale = 0.5 / math.sqrt(HD)

    def attend(q, key_tile, value_tile, q_lo, k_lo, shift, causal):
        scores = lax.dot_general(q, key_tile, (((1,), (1,)), ((), ())), preferred_element_type=jnp.float32)
        half = scores * half_scale
        act = half + half * jnp.tanh(half)
        key_pos = lax.broadcasted_iota(jnp.int32, (tile, tile), 1) + (k_lo - shift)
        first_pos = jnp.concatenate([start_ref[q_lo:q_lo + tile, :]] * (tile // HD), axis=1)
        visible = key_pos >= first_pos
        if causal:
            visible = visible & (key_pos <= lax.broadcasted_iota(jnp.int32, (tile, tile), 0) + q_lo)
        weights = jnp.where(visible, act, 0.0).astype(jnp.bfloat16)
        return jnp.dot(weights, value_tile, preferred_element_type=jnp.float32)

    def put(i, value, add):
        for part in range(tile // rows):
            at = i * (tile // rows) + part
            piece = value[part * rows:(part + 1) * rows]
            att[at] = att[at] + piece if add else piece

    for i in range(tiles):
        q = own_q[i * tile:(i + 1) * tile, :]
        acc = None
        for t in range(i + 1):
            span = slice(t * tile, (t + 1) * tile)
            term = attend(q, own_k[span, :], own_v[span, :], i * tile, t * tile, 0, t == i)
            acc = term if acc is None else acc + term
        put(i, acc, False)
    for offset in range(1, window + 1):
        @pl.when(my_ctx >= offset)
        def _():
            ctx_copy(0, own_k, prev_k, offset).wait_recv()
            ctx_copy(1, own_v, prev_v, offset).wait_recv()
            for i in range(tiles):
                q = own_q[i * tile:(i + 1) * tile, :]
                acc = None
                for t in range(i if offset == window else 0, tiles):
                    span = slice(t * tile, (t + 1) * tile)
                    term = attend(q, prev_k[offset - 1, span, :], prev_v[offset - 1, span, :],
                                  i * tile, t * tile, offset * row_count, False)
                    acc = term if acc is None else acc + term
                put(i, acc, True)

    source_other = sources[0]
    for j in range(1, per_owner):
        source_other = jnp.where(sides[j] == 1, sources[j], source_other)
    side_source = (sources[0], source_other)
    h_copies = []
    for c, (k, low, size) in enumerate(chunks):
        for m in masks:
            copies[UPDATE, c, m].wait()
        for side in range(2):
            at = jnp.int32(0)
            for j in range(per_owner):
                at = jnp.where((ranks[j] == k) & (sides[j] == side), j, at)
            rows_f32 = att[at, low:low + size, :]
            mean_square = jnp.mean(rows_f32 * rows_f32, axis=-1, keepdims=True)
            normed = rows_f32 * lax.rsqrt(mean_square + 1e-06)
            update = recv_u[c][side_source[side]].astype(jnp.float32)
            gated[c][my_head, side * size:(side + 1) * size, :] = (normed * update).astype(jnp.bfloat16)
        for offset in range(1, heads):
            copy = pltpu.make_async_remote_copy(
                src_ref=gated[c].at[my_head], dst_ref=gated[c].at[my_head],
                send_sem=h_send.at[c, offset], recv_sem=h_recv.at[c, offset],
                device_id={"head": lax.rem(my_head + offset, heads)}, device_id_type=MESH)
            copy.start()
            h_copies.append(copy)
    for copy in w_copies:
        copy.wait()
    for c, (k, low, size) in enumerate(chunks):
        for copy in h_copies[c * (heads - 1):(c + 1) * (heads - 1)]:
            copy.wait()
        acc = None
        for h in range(heads):
            term = jnp.dot(gated[c][h], w_cols[h], preferred_element_type=jnp.float32)
            acc = term if acc is None else acc + term
        acc = acc.astype(jnp.bfloat16)
        for side in range(2):
            mixed[2 * k + side, low:low + size, :] = acc[side * size:(side + 1) * size]
    for j in range(per_owner):
        out_ref[j * rows:(j + 1) * rows, :] = mixed[2 * ranks[j] + sides[j]]
    for offset in range(1, window + 1):
        @pl.when(my_ctx + offset < ctxs)
        def _():
            ctx_copy(0, own_k, prev_k, offset).wait_send()
            ctx_copy(1, own_v, prev_v, offset).wait_send()


def body(ingest, src_shard, src_slot, hist_len, w_out):
    groups, ctxs, heads = (lax.axis_size(a) for a in ("batch", "ctx", "head"))
    slot_total, rows, kinds, width = ingest.shape[2:]
    per_owner = src_shard.shape[2]
    capacity = per_owner // 2
    chunks = update_chunks(capacity, rows)
    window = ctxs // 2
    row_count = per_owner * rows
    bf16 = jnp.bfloat16
    dma = pltpu.SemaphoreType.DMA
    vmem = pl.BlockSpec(memory_space=pltpu.VMEM)
    mixed = pl.pallas_call(
        functools.partial(kernel, (groups, ctxs, heads, per_owner, rows)),
        out_shape=pltpu.VMEM((row_count, width), bf16),
        in_specs=[pl.BlockSpec(memory_space=pl.ANY)] * 5,
        out_specs=vmem,
        scratch_shapes=[
            pltpu.SMEM(src_shard.shape[1:], jnp.int32), pltpu.SMEM(src_slot.shape[1:], jnp.int32),
            pltpu.SMEM(hist_len.shape[1:], jnp.int32), pltpu.VMEM(w_out.shape, bf16), dma((4,)),
            pltpu.VMEM((slot_total, rows * kinds, width), bf16),
            pltpu.VMEM((3, groups, capacity, rows, width), bf16),
            [pltpu.VMEM((groups, size, width), bf16) for _, _, size in chunks],
            [pltpu.VMEM((groups, capacity, rows, width), bf16)] * 3,
            [pltpu.VMEM((groups, size, width), bf16) for _, _, size in chunks],
            pltpu.VMEM((row_count, width), bf16),
            pltpu.VMEM((row_count, width), bf16),
            pltpu.VMEM((row_count, width), bf16),
            pltpu.VMEM((window, row_count, width), bf16),
            pltpu.VMEM((window, row_count, width), bf16),
            pltpu.VMEM((row_count, width), jnp.int32),
            pltpu.VMEM((per_owner, rows, width), jnp.float32),
            [pltpu.VMEM((heads, 2 * size, width), bf16) for _, _, size in chunks],
            pltpu.VMEM((heads, width, width), bf16),
            pltpu.VMEM((per_owner, rows, width), bf16),
            dma((3, groups)), dma((3, groups)),
            dma((len(chunks), groups)), dma((len(chunks), groups)),
            dma((2, window)), dma((2, window)),
            dma((len(chunks), heads)), dma((len(chunks), heads)),
            dma((heads,)), dma((heads,)),
            dma, pltpu.SemaphoreType.REGULAR((groups,)), pltpu.SemaphoreType.REGULAR((groups,)),
        ],
        compiler_params=pltpu.CompilerParams(
            collective_id=0, has_side_effects=True, vmem_limit_bytes=56 * 1024 * 1024),
    )(src_shard[0], src_slot[0], hist_len[0],
      ingest.reshape(slot_total, rows * kinds, width), w_out)
    return mixed[None]


def solution(mesh):
    in_specs = (
        P("ctx", "batch", None, None, None, "head"),
        P("ctx", None, None),
        P("ctx", None, None),
        P("batch", None),
        P("head", None),
    )
    out_specs = P("batch", "ctx", "head")
    return jax.shard_map(body, mesh=mesh, in_specs=in_specs, out_specs=out_specs, check_vma=False)
```

profile of v0, /device:TPU:0, one launch (start us, length us, event | category | flops | bytes accessed | tf_op | source)
XLA Modules:
  0.0 46.3 jit_solution(7310177687811835325)
XLA Ops:
  0.0 45.6 %shard_map.55 = bf16[768,128]{1,0:T(8,128)(2,1)S(1)} custom-call(s32[4,6]{1,0:T(4,128)} %bitcast.7, s32[4,6]{1,0:T(4,128)} %bitcast.8, s32[4]{0:T(128)} %bitcast.9, bf16[12,512,128]{2,1,0:T(8,128)(2,1)} %bitcast.6, bf16[128,256]{1,0:T(8,128)(2,1)} %w_hbm.1), custom_call_target="tpu_custom_call" | custom-call | tf_op jit(solution)/shard_map/pallas_call | solution.py:324
  45.6 0.7 %copy.7 = bf16[1,768,128]{2,1,0:T(8,128)(2,1)} copy(bf16[1,768,128]{2,1,0:T(8,128)(2,1)S(1)} %bitcast.5) | data formatting | bytes 393216
where the time goes:
time: 46.5 us; the launch traced here: 46.3 us
  Pallas kernels  45.6 us (98%)
  local copies, waits for them, and re-layouts  0.68 us (1%)
    pallas_call x1, Pallas kernels, body(): pl.pallas_call(functools.partial(kernel, (groups, ctxs, heads, per_owner,...  45.6 us

commit v1 on v0

--- a/solution.py
+++ b/solution.py
@@ -14,13 +14,9 @@
 FIRST_KINDS = (KEY, VALUE, QUERY)
 
 
-def partner(me, mask, count):
-    out = 0
-    bit = 1
-    while bit < count:
-        out = out + lax.rem(lax.div(me, bit) + (mask // bit) % 2, 2) * bit
-        bit *= 2
-    return out
+def unit_list(capacity, rows):
+    units = [(kind, k) for kind in FIRST_KINDS for k in range(capacity)]
+    return units + [(UPDATE, c) for c in range(len(update_chunks(capacity, rows)))]
 
 
 def update_chunks(capacity, rows):
@@ -31,9 +27,9 @@
 def kernel(sizes, shard_hbm, slot_hbm, hist_hbm, ingest_hbm, w_hbm, out_ref,
            shard_ref, slot_ref, hist_ref, w_ref, local_sems,
            ingest_ref,
-           send_bufs, send_u, recv_bufs, recv_u, own_k, own_v, own_q, prev_k, prev_v,
+           send_bufs, send_u, recv_bufs, recv_u, relay_bufs, relay_u, own_k, own_v, own_q, prev_k, prev_v,
            start_ref, att, gated, w_cols, mixed,
-           z_send, z_recv, u_send, u_recv, c_send, c_recv, h_send, h_recv, w_send, w_recv,
+           z_send, z_recv, c_send, c_recv, h_send, h_recv, w_send, w_recv,
            ingest_sem, from_low, from_high):
     groups, ctxs, heads, per_owner, rows = sizes
     capacity = per_owner // 2
@@ -100,56 +96,117 @@
 
         return one
 
-    masks = list(range(groups - 1, 0, -1))
-    peers = {m: partner(my_group, m, groups) for m in masks}
-
-    def fill(kind):
+    units = unit_list(capacity, rows)
+    half = groups // 2
+    low_side = my_group < half
+    depth = jnp.where(low_side, half - 1 - my_group, my_group - half)
+
+    def same(e):
+        return jnp.where(low_side, half - 1 - e, half + e)
+
+    def other(e):
+        return jnp.where(low_side, half + e, half - 1 - e)
+
+    def fill(kind, k):
         one = split_kind(kind)
         for dst in range(groups):
-            for k in range(capacity):
-                if kind == UPDATE:
-                    block = one(dst, k)
-                    for c, (of, low, size) in enumerate(chunks):
-                        if of == k:
-                            send_u[c][dst] = block[low:low + size]
-                else:
-                    send_bufs[FIRST_KINDS.index(kind), dst, k] = one(dst, k)
-
-    copies = {}
-
-    def send(kind):
+            block = one(dst, k)
+            if kind == UPDATE:
+                for c, (of, low, size) in enumerate(chunks):
+                    if of == k:
+                        send_u[c][dst] = block[low:low + size]
+            else:
+                send_bufs[FIRST_KINDS.index(kind), dst, k] = block
+
+    def keep(kind):
         if kind == UPDATE:
             for c in range(len(chunks)):
-                for m in masks:
-                    copies[kind, c, m] = pltpu.make_async_remote_copy(
-                        src_ref=send_u[c].at[peers[m]], dst_ref=recv_u[c].at[my_group],
-                        send_sem=u_send.at[c, m], recv_sem=u_recv.at[c, m],
-                        device_id={"batch": peers[m]}, device_id_type=MESH)
-                    copies[kind, c, m].start()
                 recv_u[c][my_group] = send_u[c][my_group]
-            return
-        n = FIRST_KINDS.index(kind)
-        for m in masks:
-            copies[kind, m] = pltpu.make_async_remote_copy(
-                src_ref=send_bufs.at[n, peers[m]], dst_ref=recv_bufs[n].at[my_group],
-                send_sem=z_send.at[n, m], recv_sem=z_recv.at[n, m],
-                device_id={"batch": peers[m]}, device_id_type=MESH)
-            if kind != KEY:
-                copies[kind, m].start()
-        recv_bufs[n][my_group] = send_bufs[n, my_group]
+        else:
+            n = FIRST_KINDS.index(kind)
+            recv_bufs[n][my_group] = send_bufs[n, my_group]
+
+    def outbox(n, dst):
+        kind, c = units[n]
+        return send_u[c].at[dst] if kind == UPDATE else send_bufs.at[FIRST_KINDS.index(kind), dst, c]
+
+    def inbox(n, src):
+        kind, c = units[n]
+        return recv_u[c].at[src] if kind == UPDATE else recv_bufs[FIRST_KINDS.index(kind)].at[src, c]
+
+    def relay(n, far, e):
+        kind, c = units[n]
+        return relay_u[c].at[far - 1, e] if kind == UPDATE else relay_bufs[FIRST_KINDS.index(kind)].at[far - 1, e, c]
+
+    def z_copy(src, dst, n, out_id, in_id, to):
+        return pltpu.make_async_remote_copy(
+            src_ref=src, dst_ref=dst, send_sem=z_send.at[n, out_id], recv_sem=z_recv.at[n, in_id],
+            device_id={"batch": to}, device_id_type=MESH)
+
+    def side_copy(n, here, e):
+        return z_copy(outbox(n, same(e)), inbox(n, my_group), n, e, here, same(e))
+
+    def cross_copy(n, e):
+        return z_copy(outbox(n, other(e)), inbox(n, my_group), n, half + e, half, other(e))
+
+    def relay_copy(n, here, e):
+        return z_copy(outbox(n, other(e)), relay(n, here, e), n, half + e, 2 * half + (here - 1) * half + e, same(0))
+
+    def forward_copy(n, far, e):
+        return z_copy(relay(n, far, e), inbox(n, same(far)), n, 2 * half + (far - 1) * half + e, half + far, other(e))
+
+    def side(n, middle):
+        for here in range(half):
+            if (here == 0) == middle and half > 1:
+                @pl.when(depth == here)
+                def _():
+                    for e in range(half):
+                        if e != here:
+                            side_copy(n, here, e).start()
+
+    def cross(n, e):
+        @pl.when(depth == 0)
+        def _():
+            cross_copy(n, e).start()
+
+    def to_middle(n, e):
+        for here in range(1, half):
+            @pl.when(depth == here)
+            def _():
+                relay_copy(n, here, e).start()
+
+    def forward(n, e):
+        for far in range(1, half):
+            @pl.when(depth == 0)
+            def _():
+                relay_copy(n, far, e).wait_recv()
+                forward_copy(n, far, e).start()
+
+    def arrive(n):
+        for e in range(half):
+            @pl.when(depth != e)
+            def _():
+                side_copy(n, e, e).wait_recv()
+            z_copy(inbox(n, other(e)), inbox(n, other(e)), n, half + e, half + e, other(e)).wait_recv()
+
+    def sent(n):
+        for e in range(half):
+            @pl.when(depth != e)
+            def _():
+                side_copy(n, e, e).wait_send()
+            cross_copy(n, e).wait_send()
+        for far in range(1, half):
+            @pl.when(depth == 0)
+            def _():
+                for e in range(half):
+                    forward_copy(n, far, e).wait_send()
 
     def collect(kind, own_ref):
         n = FIRST_KINDS.index(kind)
-        for m in masks:
-            copies[kind, m].wait()
+        for k in range(capacity):
+            arrive(n * capacity + k)
         for j in range(per_owner):
             own_ref[j * rows:(j + 1) * rows, :] = recv_bufs[n][sources[j], ranks[j]]
-
-    def start_at(distance):
-        for m in masks:
-            @pl.when((peers[m] - my_group == distance) | (my_group - peers[m] == distance))
-            def _():
-                copies[KEY, m].start()
 
     def hear(distance):
         for there, semaphore in ((my_group >= distance, from_low), (my_group + distance < groups, from_high)):
@@ -161,24 +218,55 @@
         tell((my_group >= distance) & has_high, from_low.at[distance + 1], my_group + 1)
         tell((my_group + distance < groups) & has_low, from_high.at[distance + 1], my_group - 1)
 
+    key_units, value_units, query_units = ([n for n, (kind, _) in enumerate(units) if kind == want] for want in FIRST_KINDS)
+    update_units = list(range(3 * capacity, len(units)))
+    pairs = key_units + value_units
+    far_first = list(range(half - 1, -1, -1))
+
     ingest_copy.wait()
-    fill(KEY)
+    fill(KEY, 0)
     pl.semaphore_wait(barrier, neighbours + ctxs + heads - 2)
-    if groups > 2:
-        pass_on(1)
-    send(KEY)
-    start_at(1)
-    fill(VALUE)
-    for distance in range(2, groups):
-        hear(distance)
-        if distance + 1 < groups:
-            pass_on(distance)
-        start_at(distance)
-    send(VALUE)
-    fill(QUERY)
-    send(QUERY)
-    fill(UPDATE)
-    send(UPDATE)
+    for n in pairs:
+        if n > 0:
+            fill(*units[n])
+        if n == 1:
+            for distance in range(1, half):
+                if distance > 1:
+                    hear(distance)
+                pass_on(distance)
+        cross(n, 0)
+        to_middle(n, 0)
+        side(n, True)
+    for e in range(1, half):
+        for n in pairs:
+            to_middle(n, e)
+    for n in pairs:
+        side(n, False)
+    for n in query_units:
+        fill(QUERY, units[n][1])
+        side(n, True)
+    for k in range(capacity):
+        fill(UPDATE, k)
+    for n in update_units:
+        side(n, True)
+    for group in (query_units, update_units):
+        for e in far_first:
+            for n in group:
+                to_middle(n, e)
+        for n in group:
+            side(n, False)
+    for kind in (*FIRST_KINDS, UPDATE):
+        keep(kind)
+    if half > 1:
+        hear(half)
+    for n in pairs:
+        forward(n, 0)
+    for e in range(1, half):
+        for group in (key_units, value_units):
+            for n in group:
+                cross(n, e)
+            for n in group:
+                forward(n, e)
 
     w_copies = []
     for offset in range(1, heads):
@@ -218,6 +306,11 @@
     push(0, own_k, prev_k)
     collect(VALUE, own_v)
     push(1, own_v, prev_v)
+    for group in (query_units, update_units):
+        for e in far_first:
+            for n in group:
+                cross(n, e)
+                forward(n, e)
     collect(QUERY, own_q)
 
     tile = 2 * rows if per_owner % 2 == 0 else rows
@@ -271,17 +364,16 @@
     side_source = (sources[0], source_other)
     h_copies = []
     for c, (k, low, size) in enumerate(chunks):
-        for m in masks:
-            copies[UPDATE, c, m].wait()
-        for side in range(2):
+        arrive(update_units[c])
+        for part in range(2):
             at = jnp.int32(0)
             for j in range(per_owner):
-                at = jnp.where((ranks[j] == k) & (sides[j] == side), j, at)
+                at = jnp.where((ranks[j] == k) & (sides[j] == part), j, at)
             rows_f32 = att[at, low:low + size, :]
             mean_square = jnp.mean(rows_f32 * rows_f32, axis=-1, keepdims=True)
             normed = rows_f32 * lax.rsqrt(mean_square + 1e-06)
-            update = recv_u[c][side_source[side]].astype(jnp.float32)
-            gated[c][my_head, side * size:(side + 1) * size, :] = (normed * update).astype(jnp.bfloat16)
+            update = recv_u[c][side_source[part]].astype(jnp.float32)
+            gated[c][my_head, part * size:(part + 1) * size, :] = (normed * update).astype(jnp.bfloat16)
         for offset in range(1, heads):
             copy = pltpu.make_async_remote_copy(
                 src_ref=gated[c].at[my_head], dst_ref=gated[c].at[my_head],
@@ -291,6 +383,8 @@
             h_copies.append(copy)
     for copy in w_copies:
         copy.wait()
+    for n in range(len(units)):
+        sent(n)
     for c, (k, low, size) in enumerate(chunks):
         for copy in h_copies[c * (heads - 1):(c + 1) * (heads - 1)]:
             copy.wait()
@@ -316,6 +410,8 @@
     per_owner = src_shard.shape[2]
     capacity = per_owner // 2
     chunks = update_chunks(capacity, rows)
+    units, half = len(unit_list(capacity, rows)), groups // 2
+    spans = max(half - 1, 1)
     window = ctxs // 2
     row_count = per_owner * rows
     bf16 = jnp.bfloat16
@@ -334,6 +430,8 @@
             [pltpu.VMEM((groups, size, width), bf16) for _, _, size in chunks],
             [pltpu.VMEM((groups, capacity, rows, width), bf16)] * 3,
             [pltpu.VMEM((groups, size, width), bf16) for _, _, size in chunks],
+            [pltpu.VMEM((spans, half, capacity, rows, width), bf16)] * 3,
+            [pltpu.VMEM((spans, half, size, width), bf16) for _, _, size in chunks],
             pltpu.VMEM((row_count, width), bf16),
             pltpu.VMEM((row_count, width), bf16),
             pltpu.VMEM((row_count, width), bf16),
@@ -344,8 +442,7 @@
             [pltpu.VMEM((heads, 2 * size, width), bf16) for _, _, size in chunks],
             pltpu.VMEM((heads, width, width), bf16),
             pltpu.VMEM((per_owner, rows, width), bf16),
-            dma((3, groups)), dma((3, groups)),
-            dma((len(chunks), groups)), dma((len(chunks), groups)),
+            dma((units, groups + spans * half)), dma((units, groups + spans * half)),
             dma((2, window)), dma((2, window)),
             dma((len(chunks), heads)), dma((len(chunks), heads)),
             dma((heads,)), dma((heads,)),

time: 46.5 us -> 44.5 us (0.957)
  the two profiles are of different devices: /device:TPU:0 before, /device:TPU:8 now
where the time goes in v1:
time: 44.5 us; the launch traced here: 44.3 us
  Pallas kernels  43.6 us (98%)
  local copies, waits for them, and re-layouts  0.68 us (2%)
    pallas_call x1, Pallas kernels, body(): pl.pallas_call(functools.partial(kernel, (groups, ctxs, heads, per_owner,...  43.6 us

profile of v1, /device:TPU:8, one launch (start us, length us, event | category | flops | bytes accessed | tf_op | source)
XLA Modules:
  0.0 44.3 jit_solution(17290380990410478309)
XLA Ops:
  0.0 43.6 %shard_map.55 = bf16[768,128]{1,0:T(8,128)(2,1)S(1)} custom-call(s32[4,6]{1,0:T(4,128)} %bitcast.7, s32[4,6]{1,0:T(4,128)} %bitcast.8, s32[4]{0:T(128)} %bitcast.9, bf16[12,512,128]{2,1,0:T(8,128)(2,1)} %bitcast.6, bf16[128,256]{1,0:T(8,128)(2,1)} %w_hbm.1), custom_call_target="tpu_custom_call" | custom-call | tf_op jit(solution)/shard_map/pallas_call | solution.py:420
  43.6 0.7 %copy.7 = bf16[1,768,128]{2,1,0:T(8,128)(2,1)} copy(bf16[1,768,128]{2,1,0:T(8,128)(2,1)S(1)} %bitcast.5) | data formatting | bytes 393216

commit v2 on v1

--- a/solution.py
+++ b/solution.py
@@ -12,6 +12,8 @@
 MESH = pl.DeviceIdType.MESH
 QUERY, KEY, VALUE, UPDATE = 0, 1, 2, 3
 FIRST_KINDS = (KEY, VALUE, QUERY)
+KINDS = (*FIRST_KINDS, UPDATE)
+SPREAD = ((9,3),(8,0))
 
 
 def unit_list(capacity, rows):
@@ -20,14 +22,17 @@
 
 
 def update_chunks(capacity, rows):
-    half = rows // 2
-    return [(k, 0, rows) for k in range(capacity - 1)] + [(capacity - 1, 0, half), (capacity - 1, half, half)]
+    chunks, low = [(k, 0, rows) for k in range(capacity - 1)], 0
+    for share in (2,4,4):
+        chunks.append((capacity - 1, low, rows // share))
+        low += rows // share
+    return chunks
 
 
 def kernel(sizes, shard_hbm, slot_hbm, hist_hbm, ingest_hbm, w_hbm, out_ref,
            shard_ref, slot_ref, hist_ref, w_ref, local_sems,
            ingest_ref,
-           send_bufs, send_u, recv_bufs, recv_u, relay_bufs, relay_u, own_k, own_v, own_q, prev_k, prev_v,
+           send_buf, recv_bufs, recv_u, relay_buf, own_k, own_v, own_q, prev_k, prev_v,
            start_ref, att, gated, w_cols, mixed,
            z_send, z_recv, c_send, c_recv, h_send, h_recv, w_send, w_recv,
            ingest_sem, from_low, from_high):
@@ -109,51 +114,49 @@
 
     def fill(kind, k):
         one = split_kind(kind)
+        low = (KINDS.index(kind) * capacity + k) * rows
         for dst in range(groups):
-            block = one(dst, k)
-            if kind == UPDATE:
-                for c, (of, low, size) in enumerate(chunks):
-                    if of == k:
-                        send_u[c][dst] = block[low:low + size]
-            else:
-                send_bufs[FIRST_KINDS.index(kind), dst, k] = block
-
-    def keep(kind):
-        if kind == UPDATE:
-            for c in range(len(chunks)):
-                recv_u[c][my_group] = send_u[c][my_group]
-        else:
-            n = FIRST_KINDS.index(kind)
-            recv_bufs[n][my_group] = send_bufs[n, my_group]
-
-    def outbox(n, dst):
+            send_buf[dst, low:low + rows, :] = one(dst, k)
+
+    def span(n):
         kind, c = units[n]
-        return send_u[c].at[dst] if kind == UPDATE else send_bufs.at[FIRST_KINDS.index(kind), dst, c]
+        k, low, size = chunks[c] if kind == UPDATE else (c, 0, rows)
+        return pl.ds((KINDS.index(kind) * capacity + k) * rows + low, size)
 
     def inbox(n, src):
         kind, c = units[n]
         return recv_u[c].at[src] if kind == UPDATE else recv_bufs[FIRST_KINDS.index(kind)].at[src, c]
 
-    def relay(n, far, e):
+    def keep(kind):
+        for n, (of, _) in enumerate(units):
+            if of == kind:
+                inbox(n, my_group)[...] = send_buf[my_group, span(n), :]
+
+    def z_copy(src, dst, out_id, in_id, to):
+        return pltpu.make_async_remote_copy(
+            src_ref=src, dst_ref=dst, send_sem=z_send.at[out_id], recv_sem=z_recv.at[in_id],
+            device_id={"batch": to}, device_id_type=MESH)
+
+    def here_id(n):
         kind, c = units[n]
-        return relay_u[c].at[far - 1, e] if kind == UPDATE else relay_bufs[FIRST_KINDS.index(kind)].at[far - 1, e, c]
-
-    def z_copy(src, dst, n, out_id, in_id, to):
-        return pltpu.make_async_remote_copy(
-            src_ref=src, dst_ref=dst, send_sem=z_send.at[n, out_id], recv_sem=z_recv.at[n, in_id],
-            device_id={"batch": to}, device_id_type=MESH)
-
-    def side_copy(n, here, e):
-        return z_copy(outbox(n, same(e)), inbox(n, my_group), n, e, here, same(e))
+        return 3 + c if kind == UPDATE else FIRST_KINDS.index(kind)
+
+    def relay_id(kind, far, e):
+        return 3 + len(chunks) + (KINDS.index(kind) * (half - 1) + far - 1) * half + e
+
+    def side_copy(n, e):
+        return z_copy(send_buf.at[same(e), span(n)], inbox(n, my_group), e, here_id(n), same(e))
 
     def cross_copy(n, e):
-        return z_copy(outbox(n, other(e)), inbox(n, my_group), n, half + e, half, other(e))
-
-    def relay_copy(n, here, e):
-        return z_copy(outbox(n, other(e)), relay(n, here, e), n, half + e, 2 * half + (here - 1) * half + e, same(0))
+        return z_copy(send_buf.at[other(e), span(n)], inbox(n, my_group), half + e, here_id(n), other(e))
+
+    def relay_copy(n, far, e):
+        return z_copy(send_buf.at[other(e), span(n)], relay_buf.at[far - 1, e, span(n)],
+                      half + e, relay_id(units[n][0], far, e), same(0))
 
     def forward_copy(n, far, e):
-        return z_copy(relay(n, far, e), inbox(n, same(far)), n, 2 * half + (far - 1) * half + e, half + far, other(e))
+        return z_copy(relay_buf.at[far - 1, e, span(n)], inbox(n, same(far)),
+                      2 * half + (far - 1) * half + e, here_id(n), other(e))
 
     def side(n, middle):
         for here in range(half):
@@ -162,7 +165,7 @@
                 def _():
                     for e in range(half):
                         if e != here:
-                            side_copy(n, here, e).start()
+                            side_copy(n, e).start()
 
     def cross(n, e):
         @pl.when(depth == 0)
@@ -175,36 +178,39 @@
             def _():
                 relay_copy(n, here, e).start()
 
+    relayed = set()
+
     def forward(n, e):
+        kind = units[n][0]
+        first = (kind, e) not in relayed
+        relayed.add((kind, e))
         for far in range(1, half):
             @pl.when(depth == 0)
             def _():
-                relay_copy(n, far, e).wait_recv()
+                if first:
+                    whole = relay_buf.at[far - 1, e, pl.ds(KINDS.index(kind) * capacity * rows, capacity * rows)]
+                    z_copy(whole, whole, 0, relay_id(kind, far, e), my_group).wait_recv()
                 forward_copy(n, far, e).start()
 
-    def arrive(n):
+    def arrive(buf, in_id):
+        others = buf.at[pl.ds(0, groups - 1)]
+        z_copy(others, others, 0, in_id, my_group).wait_recv()
+
+    def sent():
+        whole = send_buf.at[0]
         for e in range(half):
             @pl.when(depth != e)
             def _():
-                side_copy(n, e, e).wait_recv()
-            z_copy(inbox(n, other(e)), inbox(n, other(e)), n, half + e, half + e, other(e)).wait_recv()
-
-    def sent(n):
-        for e in range(half):
-            @pl.when(depth != e)
-            def _():
-                side_copy(n, e, e).wait_send()
-            cross_copy(n, e).wait_send()
-        for far in range(1, half):
+                z_copy(whole, whole, e, 0, my_group).wait_send()
+            z_copy(whole, whole, half + e, 0, my_group).wait_send()
+        for flow in range(2 * half, half + half * half):
             @pl.when(depth == 0)
             def _():
-                for e in range(half):
-                    forward_copy(n, far, e).wait_send()
+                z_copy(whole, whole, flow, 0, my_group).wait_send()
 
     def collect(kind, own_ref):
         n = FIRST_KINDS.index(kind)
-        for k in range(capacity):
-            arrive(n * capacity + k)
+        arrive(recv_bufs[n], n)
         for j in range(per_owner):
             own_ref[j * rows:(j + 1) * rows, :] = recv_bufs[n][sources[j], ranks[j]]
 
@@ -212,16 +218,21 @@
         for there, semaphore in ((my_group >= distance, from_low), (my_group + distance < groups, from_high)):
             @pl.when(there)
             def _():
-                pl.semaphore_wait(semaphore.at[distance], 1)
+                pl.semaphore_wait(semaphore.at[distance - 2], 1)
 
     def pass_on(distance):
-        tell((my_group >= distance) & has_high, from_low.at[distance + 1], my_group + 1)
-        tell((my_group + distance < groups) & has_low, from_high.at[distance + 1], my_group - 1)
+        tell((my_group >= distance) & has_high, from_low.at[distance - 1], my_group + 1)
+        tell((my_group + distance < groups) & has_low, from_high.at[distance - 1], my_group - 1)
 
     key_units, value_units, query_units = ([n for n, (kind, _) in enumerate(units) if kind == want] for want in FIRST_KINDS)
     update_units = list(range(3 * capacity, len(units)))
     pairs = key_units + value_units
     far_first = list(range(half - 1, -1, -1))
+    query_order = [(n, e) for e in far_first for n in query_units]
+    ends_at = [(chunks[c][0] + (chunks[c][1] + chunks[c][2]) / rows) / capacity for c in range(len(chunks))]
+    update_order = sorted(
+        ((n, e) for n in update_units for e in far_first),
+        key=lambda one: ends_at[one[0] - update_units[0]] * SPREAD[one[1] > 0][0] + SPREAD[one[1] > 0][1])
 
     ingest_copy.wait()
     fill(KEY, 0)
@@ -249,13 +260,12 @@
         fill(UPDATE, k)
     for n in update_units:
         side(n, True)
-    for group in (query_units, update_units):
-        for e in far_first:
-            for n in group:
-                to_middle(n, e)
+    for group, sequence in ((query_units, query_order), (update_units, update_order)):
+        for n, e in sequence:
+            to_middle(n, e)
         for n in group:
             side(n, False)
-    for kind in (*FIRST_KINDS, UPDATE):
+    for kind in KINDS:
         keep(kind)
     if half > 1:
         hear(half)
@@ -273,7 +283,7 @@
         to = lax.rem(my_head + offset, heads)
         copy = pltpu.make_async_remote_copy(
             src_ref=w_ref.at[:, pl.ds(pl.multiple_of(to * HD, HD), HD)], dst_ref=w_cols.at[my_head],
-            send_sem=w_send.at[offset], recv_sem=w_recv.at[offset],
+            send_sem=w_send.at[offset - 1], recv_sem=w_recv,
             device_id={"head": to}, device_id_type=MESH)
         copy.start()
         w_copies.append(copy)
@@ -306,11 +316,9 @@
     push(0, own_k, prev_k)
     collect(VALUE, own_v)
     push(1, own_v, prev_v)
-    for group in (query_units, update_units):
-        for e in far_first:
-            for n in group:
-                cross(n, e)
-                forward(n, e)
+    for n, e in query_order + update_order:
+        cross(n, e)
+        forward(n, e)
     collect(QUERY, own_q)
 
     tile = 2 * rows if per_owner % 2 == 0 else rows
@@ -362,9 +370,8 @@
     for j in range(1, per_owner):
         source_other = jnp.where(sides[j] == 1, sources[j], source_other)
     side_source = (sources[0], source_other)
-    h_copies = []
     for c, (k, low, size) in enumerate(chunks):
-        arrive(update_units[c])
+        arrive(recv_u[c], 3 + c)
         for part in range(2):
             at = jnp.int32(0)
             for j in range(per_owner):
@@ -377,17 +384,19 @@
         for offset in range(1, heads):
             copy = pltpu.make_async_remote_copy(
                 src_ref=gated[c].at[my_head], dst_ref=gated[c].at[my_head],
-                send_sem=h_send.at[c, offset], recv_sem=h_recv.at[c, offset],
+                send_sem=h_send.at[offset - 1], recv_sem=h_recv.at[c],
                 device_id={"head": lax.rem(my_head + offset, heads)}, device_id_type=MESH)
             copy.start()
-            h_copies.append(copy)
     for copy in w_copies:
-        copy.wait()
-    for n in range(len(units)):
-        sent(n)
+        copy.wait_send()
+    if heads > 1:
+        all_cols = w_cols.at[pl.ds(0, heads - 1)]
+        pltpu.make_async_copy(all_cols, all_cols, w_recv).wait()
+    sent()
     for c, (k, low, size) in enumerate(chunks):
-        for copy in h_copies[c * (heads - 1):(c + 1) * (heads - 1)]:
-            copy.wait()
+        if heads > 1:
+            theirs = gated[c].at[pl.ds(0, heads - 1)]
+            pltpu.make_async_copy(theirs, theirs, h_recv.at[c]).wait()
         acc = None
         for h in range(heads):
             term = jnp.dot(gated[c][h], w_cols[h], preferred_element_type=jnp.float32)
@@ -395,6 +404,10 @@
         acc = acc.astype(jnp.bfloat16)
         for side in range(2):
             mixed[2 * k + side, low:low + size, :] = acc[side * size:(side + 1) * size]
+    for offset in range(1, heads):
+        pltpu.make_async_remote_copy(
+            src_ref=own_q, dst_ref=own_q, send_sem=h_send.at[offset - 1], recv_sem=h_recv.at[0],
+            device_id={"head": my_head}, device_id_type=MESH).wait_send()
     for j in range(per_owner):
         out_ref[j * rows:(j + 1) * rows, :] = mixed[2 * ranks[j] + sides[j]]
     for offset in range(1, window + 1):
@@ -410,7 +423,7 @@
     per_owner = src_shard.shape[2]
     capacity = per_owner // 2
     chunks = update_chunks(capacity, rows)
-    units, half = len(unit_list(capacity, rows)), groups // 2
+    half = groups // 2
     spans = max(half - 1, 1)
     window = ctxs // 2
     row_count = per_owner * rows
@@ -426,12 +439,10 @@
             pltpu.SMEM(src_shard.shape[1:], jnp.int32), pltpu.SMEM(src_slot.shape[1:], jnp.int32),
             pltpu.SMEM(hist_len.shape[1:], jnp.int32), pltpu.VMEM(w_out.shape, bf16), dma((4,)),
             pltpu.VMEM((slot_total, rows * kinds, width), bf16),
-            pltpu.VMEM((3, groups, capacity, rows, width), bf16),
-            [pltpu.VMEM((groups, size, width), bf16) for _, _, size in chunks],
+            pltpu.VMEM((groups, 4 * capacity * rows, width), bf16),
             [pltpu.VMEM((groups, capacity, rows, width), bf16)] * 3,
             [pltpu.VMEM((groups, size, width), bf16) for _, _, size in chunks],
-            [pltpu.VMEM((spans, half, capacity, rows, width), bf16)] * 3,
-            [pltpu.VMEM((spans, half, size, width), bf16) for _, _, size in chunks],
+            pltpu.VMEM((spans, half, 4 * capacity * rows, width), bf16),
             pltpu.VMEM((row_count, width), bf16),
             pltpu.VMEM((row_count, width), bf16),
             pltpu.VMEM((row_count, width), bf16),
@@ -442,11 +453,11 @@
             [pltpu.VMEM((heads, 2 * size, width), bf16) for _, _, size in chunks],
             pltpu.VMEM((heads, width, width), bf16),
             pltpu.VMEM((per_owner, rows, width), bf16),
-            dma((units, groups + spans * half)), dma((units, groups + spans * half)),
+            dma((groups + spans * half,)), dma((3 + len(chunks) + 4 * spans * half,)),
             dma((2, window)), dma((2, window)),
-            dma((len(chunks), heads)), dma((len(chunks), heads)),
-            dma((heads,)), dma((heads,)),
-            dma, pltpu.SemaphoreType.REGULAR((groups,)), pltpu.SemaphoreType.REGULAR((groups,)),
+            dma((max(heads - 1, 1),)), dma((len(chunks),)),
+            dma((max(heads - 1, 1),)), dma,
+            dma, pltpu.SemaphoreType.REGULAR((spans,)), pltpu.SemaphoreType.REGULAR((spans,)),
         ],
         compiler_params=pltpu.CompilerParams(
             collective_id=0, has_side_effects=True, vmem_limit_bytes=56 * 1024 * 1024),

time: 44.5 us -> 44 us (0.989)
  Pallas kernels: 43.6 us -> 42.9 us
    pallas_call x1, Pallas kernels: 43.6 us -> 42.9 us  [body(): pl.pallas_call(functools.partial(kernel, (groups, ctxs, heads, per_owner,...]
where the time goes in v2:
time: 44 us; the launch traced here: 43.6 us
  Pallas kernels  42.9 us (98%)
  local copies, waits for them, and re-layouts  0.68 us (2%)
    pallas_call x1, Pallas kernels, body(): pl.pallas_call(functools.partial(kernel, (groups, ctxs, heads, per_owner,...  42.9 us

profile of v2, /device:TPU:8, one launch (start us, length us, event | category | flops | bytes accessed | tf_op | source)
XLA Modules:
  0.0 43.6 jit_solution(9465711823678424650)
XLA Ops:
  0.0 42.9 %shard_map.55 = bf16[768,128]{1,0:T(8,128)(2,1)S(1)} custom-call(s32[4,6]{1,0:T(4,128)} %bitcast.7, s32[4,6]{1,0:T(4,128)} %bitcast.8, s32[4]{0:T(128)} %bitcast.9, bf16[12,512,128]{2,1,0:T(8,128)(2,1)} %bitcast.6, bf16[128,256]{1,0:T(8,128)(2,1)} %w_hbm.1), custom_call_target="tpu_custom_call" | custom-call | tf_op jit(solution)/shard_map/pallas_call | solution.py:433
  42.9 0.7 %copy.7 = bf16[1,768,128]{2,1,0:T(8,128)(2,1)} copy(bf16[1,768,128]{2,1,0:T(8,128)(2,1)S(1)} %bitcast.5) | data formatting | bytes 393216

commit v3 on v2

--- a/solution.py
+++ b/solution.py
@@ -228,6 +228,7 @@
     update_units = list(range(3 * capacity, len(units)))
     pairs = key_units + value_units
     far_first = list(range(half - 1, -1, -1))
+    early = [(n, 0) for n in query_units]
     query_order = [(n, e) for e in far_first for n in query_units]
     ends_at = [(chunks[c][0] + (chunks[c][1] + chunks[c][2]) / rows) / capacity for c in range(len(chunks))]
     update_order = sorted(
@@ -255,6 +256,7 @@
         side(n, False)
     for n in query_units:
         fill(QUERY, units[n][1])
+        cross(n, 0)
         side(n, True)
     for k in range(capacity):
         fill(UPDATE, k)
@@ -317,7 +319,8 @@
     collect(VALUE, own_v)
     push(1, own_v, prev_v)
     for n, e in query_order + update_order:
-        cross(n, e)
+        if (n, e) not in early:
+            cross(n, e)
         forward(n, e)
     collect(QUERY, own_q)
 

time: 44 us -> 43.1 us (0.980)
  Pallas kernels: 42.9 us -> 42.2 us
    pallas_call x1, Pallas kernels: 42.9 us -> 42.2 us  [body(): pl.pallas_call(functools.partial(kernel, (groups, ctxs, heads, per_owner,...]
where the time goes in v3:
time: 43.1 us; the launch traced here: 42.9 us
  Pallas kernels  42.2 us (98%)
  local copies, waits for them, and re-layouts  0.68 us (2%)
    pallas_call x1, Pallas kernels, body(): pl.pallas_call(functools.partial(kernel, (groups, ctxs, heads, per_owner,...  42.2 us

profile of v3, /device:TPU:8, one launch (start us, length us, event | category | flops | bytes accessed | tf_op | source)
XLA Modules:
  0.0 42.9 jit_solution(1580905787041136973)
XLA Ops:
  0.0 42.2 %shard_map.55 = bf16[768,128]{1,0:T(8,128)(2,1)S(1)} custom-call(s32[4,6]{1,0:T(4,128)} %bitcast.7, s32[4,6]{1,0:T(4,128)} %bitcast.8, s32[4]{0:T(128)} %bitcast.9, bf16[12,512,128]{2,1,0:T(8,128)(2,1)} %bitcast.6, bf16[128,256]{1,0:T(8,128)(2,1)} %w_hbm.1), custom_call_target="tpu_custom_call" | custom-call | tf_op jit(solution)/shard_map/pallas_call | solution.py:436
  42.2 0.7 %copy.7 = bf16[1,768,128]{2,1,0:T(8,128)(2,1)} copy(bf16[1,768,128]{2,1,0:T(8,128)(2,1)S(1)} %bitcast.5) | data formatting | bytes 393216

commit v4 on v3

--- a/solution.py
+++ b/solution.py
@@ -13,29 +13,40 @@
 QUERY, KEY, VALUE, UPDATE = 0, 1, 2, 3
 FIRST_KINDS = (KEY, VALUE, QUERY)
 KINDS = (*FIRST_KINDS, UPDATE)
-SPREAD = ((9,3),(8,0))
+SPREAD = ((9,3),(7,0))
+NEAR_QUERY = -0.5
+NEAR_FIRST = 2.4
+SPLITS = ((1,),(2,2),(2,4,4))
+
+
+def load_pieces(rows):
+    return [(0, rows // 4), (rows // 4, rows - rows // 4)]
 
 
 def unit_list(capacity, rows):
-    units = [(kind, k) for kind in FIRST_KINDS for k in range(capacity)]
-    return units + [(UPDATE, c) for c in range(len(update_chunks(capacity, rows)))]
+    units = [(KEY, 0, 0, low, size) for low, size in load_pieces(rows)]
+    units += [(KEY, k, k, 0, rows) for k in range(1, capacity)]
+    units += [(kind, k, k, 0, rows) for kind in FIRST_KINDS[1:] for k in range(capacity)]
+    return units + [(UPDATE, c, *chunk) for c, chunk in enumerate(update_chunks(capacity, rows))]
 
 
 def update_chunks(capacity, rows):
-    chunks, low = [(k, 0, rows) for k in range(capacity - 1)], 0
-    for share in (2,4,4):
-        chunks.append((capacity - 1, low, rows // share))
-        low += rows // share
+    chunks = []
+    for k in range(capacity):
+        low = 0
+        for share in SPLITS[max(k + len(SPLITS) - capacity, 0)]:
+            chunks.append((k, low, rows // share))
+            low += rows // share
     return chunks
 
 
 def kernel(sizes, shard_hbm, slot_hbm, hist_hbm, ingest_hbm, w_hbm, out_ref,
            shard_ref, slot_ref, hist_ref, w_ref, local_sems,
-           ingest_ref,
+           ingest_refs,
            send_buf, recv_bufs, recv_u, relay_buf, own_k, own_v, own_q, prev_k, prev_v,
            start_ref, att, gated, w_cols, mixed,
            z_send, z_recv, c_send, c_recv, h_send, h_recv, w_send, w_recv,
-           ingest_sem, from_low, from_high):
+           ingest_sems, from_low, from_high):
     groups, ctxs, heads, per_owner, rows = sizes
     capacity = per_owner // 2
     chunks = update_chunks(capacity, rows)
@@ -46,11 +57,14 @@
     my_head = lax.axis_index("head")
 
     barrier = pltpu.get_barrier_semaphore()
-    ingest_copy = pltpu.make_async_copy(ingest_hbm, ingest_ref, ingest_sem)
-    ingest_copy.start()
     local_copies = [pltpu.make_async_copy(src, dst, local_sems.at[i]) for i, (src, dst) in enumerate((
         (shard_hbm, shard_ref), (slot_hbm, slot_ref), (hist_hbm, hist_ref), (w_hbm, w_ref)))]
-    for copy in local_copies:
+    pieces = load_pieces(rows)
+    kinds = ingest_hbm.shape[1] // rows
+    ingest_copies = [pltpu.make_async_copy(
+        ingest_hbm.at[:, pl.ds(low * kinds, size * kinds), :], ingest_refs[p], ingest_sems.at[p])
+        for p, (low, size) in enumerate(pieces)]
+    for copy in (*local_copies[:2], *ingest_copies, *local_copies[2:]):
         copy.start()
     for axis, me, count in (("ctx", my_ctx, ctxs), ("head", my_head, heads)):
         for offset in range(1, count):
@@ -66,7 +80,7 @@
     tell(has_high, barrier, my_group + 1)
     neighbours = jnp.where(has_low, 1, 0) + jnp.where(has_high, 1, 0)
 
-    for copy in local_copies:
+    for copy in local_copies[:2]:
         copy.wait()
     slots = []
     for dst in range(groups):
@@ -89,14 +103,17 @@
         ranks.append(jnp.minimum(rank, capacity - 1))
         sides.append(jnp.where(sources[j] == sources[0], 0, 1))
 
+    fine = rows // 4
+
     def split_kind(kind):
-        width = 4 * rows
-        row = lax.broadcasted_iota(jnp.int32, (rows, width), 0)
-        col = lax.broadcasted_iota(jnp.int32, (rows, width), 1)
-        pick = jnp.where(col == row * 4 + kind, 1.0, 0.0).astype(jnp.bfloat16)
-
-        def one(dst, k):
-            block = ingest_ref[slots[dst][k]]
+        row = lax.broadcasted_iota(jnp.int32, (fine, fine * kinds), 0)
+        col = lax.broadcasted_iota(jnp.int32, (fine, fine * kinds), 1)
+        pick = jnp.where(col == row * kinds + kind, 1.0, 0.0).astype(jnp.bfloat16)
+
+        def one(dst, k, low):
+            p = max(p for p, (first, _) in enumerate(pieces) if first <= low)
+            at = (low - pieces[p][0]) * kinds
+            block = ingest_refs[p][slots[dst][k], at:at + fine * kinds, :]
             return jnp.dot(pick, block, preferred_element_type=jnp.float32).astype(jnp.bfloat16)
 
         return one
@@ -112,24 +129,24 @@
     def other(e):
         return jnp.where(low_side, half + e, half - 1 - e)
 
-    def fill(kind, k):
+    def fill(kind, k, low, size):
         one = split_kind(kind)
-        low = (KINDS.index(kind) * capacity + k) * rows
+        base = (KINDS.index(kind) * capacity + k) * rows
         for dst in range(groups):
-            send_buf[dst, low:low + rows, :] = one(dst, k)
+            for at in range(low, low + size, fine):
+                send_buf[dst, base + at:base + at + fine, :] = one(dst, k, at)
 
     def span(n):
-        kind, c = units[n]
-        k, low, size = chunks[c] if kind == UPDATE else (c, 0, rows)
+        kind, _, k, low, size = units[n]
         return pl.ds((KINDS.index(kind) * capacity + k) * rows + low, size)
 
     def inbox(n, src):
-        kind, c = units[n]
-        return recv_u[c].at[src] if kind == UPDATE else recv_bufs[FIRST_KINDS.index(kind)].at[src, c]
+        kind, c, k, low, size = units[n]
+        return recv_u[c].at[src] if kind == UPDATE else recv_bufs[FIRST_KINDS.index(kind)].at[src, k, pl.ds(low, size)]
 
     def keep(kind):
-        for n, (of, _) in enumerate(units):
-            if of == kind:
+        for n, unit in enumerate(units):
+            if unit[0] == kind:
                 inbox(n, my_group)[...] = send_buf[my_group, span(n), :]
 
     def z_copy(src, dst, out_id, in_id, to):
@@ -138,7 +155,7 @@
             device_id={"batch": to}, device_id_type=MESH)
 
     def here_id(n):
-        kind, c = units[n]
+        kind, c = units[n][:2]
         return 3 + c if kind == UPDATE else FIRST_KINDS.index(kind)
 
     def relay_id(kind, far, e):
@@ -224,54 +241,66 @@
         tell((my_group >= distance) & has_high, from_low.at[distance - 1], my_group + 1)
         tell((my_group + distance < groups) & has_low, from_high.at[distance - 1], my_group - 1)
 
-    key_units, value_units, query_units = ([n for n, (kind, _) in enumerate(units) if kind == want] for want in FIRST_KINDS)
-    update_units = list(range(3 * capacity, len(units)))
+    key_units, value_units, query_units = ([n for n, unit in enumerate(units) if unit[0] == want] for want in FIRST_KINDS)
+    update_units = [n for n, unit in enumerate(units) if unit[0] == UPDATE]
     pairs = key_units + value_units
     far_first = list(range(half - 1, -1, -1))
     early = [(n, 0) for n in query_units]
-    query_order = [(n, e) for e in far_first for n in query_units]
-    ends_at = [(chunks[c][0] + (chunks[c][1] + chunks[c][2]) / rows) / capacity for c in range(len(chunks))]
-    update_order = sorted(
-        ((n, e) for n in update_units for e in far_first),
-        key=lambda one: ends_at[one[0] - update_units[0]] * SPREAD[one[1] > 0][0] + SPREAD[one[1] > 0][1])
-
-    ingest_copy.wait()
-    fill(KEY, 0)
+    ends_at = [(k + (low + size) / rows) / capacity for k, low, size in chunks]
+
+    def turn(one):
+        n, e = one
+        if n in query_units:
+            return NEAR_QUERY if e == 0 else -1
+        if (n, e) == (update_units[0], 0):
+            return NEAR_FIRST
+        slope, first = SPREAD[e > 0]
+        return ends_at[n - update_units[0]] * slope + first
+
+    late_order = sorted([(n, e) for n in query_units + update_units for e in far_first], key=turn)
+
+    ingest_copies[0].wait()
+    fill(KEY, *units[0][2:])
     pl.semaphore_wait(barrier, neighbours + ctxs + heads - 2)
     for n in pairs:
+        if n == 1:
+            for copy in ingest_copies[1:]:
+                copy.wait()
         if n > 0:
-            fill(*units[n])
+            fill(units[n][0], *units[n][2:])
         if n == 1:
             for distance in range(1, half):
                 if distance > 1:
                     hear(distance)
                 pass_on(distance)
         cross(n, 0)
-        to_middle(n, 0)
+        if n in key_units:
+            to_middle(n, 0)
         side(n, True)
     for e in range(1, half):
         for n in pairs:
             to_middle(n, e)
+    for n in value_units:
+        to_middle(n, 0)
     for n in pairs:
         side(n, False)
     for n in query_units:
-        fill(QUERY, units[n][1])
+        fill(QUERY, *units[n][2:])
         cross(n, 0)
         side(n, True)
     for k in range(capacity):
-        fill(UPDATE, k)
+        fill(UPDATE, k, 0, rows)
     for n in update_units:
         side(n, True)
-    for group, sequence in ((query_units, query_order), (update_units, update_order)):
-        for n, e in sequence:
-            to_middle(n, e)
-        for n in group:
-            side(n, False)
+    for n, e in late_order:
+        to_middle(n, e)
+    for n in query_units + update_units:
+        side(n, False)
     for kind in KINDS:
         keep(kind)
     if half > 1:
         hear(half)
-    for n in pairs:
+    for n in key_units:
         forward(n, 0)
     for e in range(1, half):
         for group in (key_units, value_units):
@@ -279,7 +308,11 @@
                 cross(n, e)
             for n in group:
                 forward(n, e)
-
+    for n in value_units:
+        forward(n, 0)
+
+    for copy in local_copies[2:]:
+        copy.wait()
     w_copies = []
     for offset in range(1, heads):
         to = lax.rem(my_head + offset, heads)
@@ -316,9 +349,15 @@
 
     collect(KEY, own_k)
     push(0, own_k, prev_k)
+    for n, e in late_order:
+        if n in query_units and e > 0:
+            cross(n, e)
+            forward(n, e)
     collect(VALUE, own_v)
     push(1, own_v, prev_v)
-    for n, e in query_order + update_order:
+    for n, e in late_order:
+        if n in query_units and e > 0:
+            continue
         if (n, e) not in early:
             cross(n, e)
         forward(n, e)
@@ -441,7 +480,7 @@
         scratch_shapes=[
             pltpu.SMEM(src_shard.shape[1:], jnp.int32), pltpu.SMEM(src_slot.shape[1:], jnp.int32),
             pltpu.SMEM(hist_len.shape[1:], jnp.int32), pltpu.VMEM(w_out.shape, bf16), dma((4,)),
-            pltpu.VMEM((slot_total, rows * kinds, width), bf16),
+            [pltpu.VMEM((slot_total, size * kinds, width), bf16) for _, size in load_pieces(rows)],
             pltpu.VMEM((groups, 4 * capacity * rows, width), bf16),
             [pltpu.VMEM((groups, capacity, rows, width), bf16)] * 3,
             [pltpu.VMEM((groups, size, width), bf16) for _, _, size in chunks],
@@ -460,7 +499,7 @@
             dma((2, window)), dma((2, window)),
             dma((max(heads - 1, 1),)), dma((len(chunks),)),
             dma((max(heads - 1, 1),)), dma,
-            dma, pltpu.SemaphoreType.REGULAR((spans,)), pltpu.SemaphoreType.REGULAR((spans,)),
+            dma((2,)), pltpu.SemaphoreType.REGULAR((spans,)), pltpu.SemaphoreType.REGULAR((spans,)),
         ],
         compiler_params=pltpu.CompilerParams(
             collective_id=0, has_side_effects=True, vmem_limit_bytes=56 * 1024 * 1024),

time: 43.1 us -> 42.9 us (level)
  no operation moved by 1% of the time
where the time goes in v4:
time: 42.9 us; the launch traced here: 42.7 us
  Pallas kernels  42 us (98%)
  local copies, waits for them, and re-layouts  0.68 us (2%)
    pallas_call x1, Pallas kernels, body(): pl.pallas_call(functools.partial(kernel, (groups, ctxs, heads, per_owner,...  42 us

profile of v4, /device:TPU:8, one launch (start us, length us, event | category | flops | bytes accessed | tf_op | source)
XLA Modules:
  0.0 42.7 jit_solution(16873080684293126745)
XLA Ops:
  0.0 42.0 %shard_map.55 = bf16[768,128]{1,0:T(8,128)(2,1)S(1)} custom-call(s32[4,6]{1,0:T(4,128)} %bitcast.7, s32[4,6]{1,0:T(4,128)} %bitcast.8, s32[4]{0:T(128)} %bitcast.9, bf16[12,512,128]{2,1,0:T(8,128)(2,1)} %bitcast.6, bf16[128,256]{1,0:T(8,128)(2,1)} %w_hbm.1), custom_call_target="tpu_custom_call" | custom-call | tf_op jit(solution)/shard_map/pallas_call | solution.py:475
  42.0 0.7 %copy.7 = bf16[1,768,128]{2,1,0:T(8,128)(2,1)} copy(bf16[1,768,128]{2,1,0:T(8,128)(2,1)S(1)} %bitcast.5) | data formatting | bytes 393216

commit v5 on v4

--- a/solution.py
+++ b/solution.py
@@ -13,10 +13,7 @@
 QUERY, KEY, VALUE, UPDATE = 0, 1, 2, 3
 FIRST_KINDS = (KEY, VALUE, QUERY)
 KINDS = (*FIRST_KINDS, UPDATE)
-SPREAD = ((9,3),(7,0))
-NEAR_QUERY = -0.5
-NEAR_FIRST = 2.4
-SPLITS = ((1,),(2,2),(2,4,4))
+SPLIT = 2
 
 
 def load_pieces(rows):
@@ -31,13 +28,8 @@
 
 
 def update_chunks(capacity, rows):
-    chunks = []
-    for k in range(capacity):
-        low = 0
-        for share in SPLITS[max(k + len(SPLITS) - capacity, 0)]:
-            chunks.append((k, low, rows // share))
-            low += rows // share
-    return chunks
+    size = rows // SPLIT
+    return [(k, part * size, size) for k in range(capacity) for part in range(SPLIT)]
 
 
 def kernel(sizes, shard_hbm, slot_hbm, hist_hbm, ingest_hbm, w_hbm, out_ref,
@@ -246,18 +238,7 @@
     pairs = key_units + value_units
     far_first = list(range(half - 1, -1, -1))
     early = [(n, 0) for n in query_units]
-    ends_at = [(k + (low + size) / rows) / capacity for k, low, size in chunks]
-
-    def turn(one):
-        n, e = one
-        if n in query_units:
-            return NEAR_QUERY if e == 0 else -1
-        if (n, e) == (update_units[0], 0):
-            return NEAR_FIRST
-        slope, first = SPREAD[e > 0]
-        return ends_at[n - update_units[0]] * slope + first
-
-    late_order = sorted([(n, e) for n in query_units + update_units for e in far_first], key=turn)
+    late_order = [(n, e) for group in (query_units, update_units) for e in far_first for n in group]
 
     ingest_copies[0].wait()
     fill(KEY, *units[0][2:])

time: 42.9 us -> 42.9 us (level)
  no operation moved by 1% of the time
where the time goes in v5:
time: 42.9 us; the launch traced here: 42.7 us
  Pallas kernels  42 us (98%)
  local copies, waits for them, and re-layouts  0.68 us (2%)
    pallas_call x1, Pallas kernels, body(): pl.pallas_call(functools.partial(kernel, (groups, ctxs, heads, per_owner,...  42 us

profile of v5, /device:TPU:8, one launch (start us, length us, event | category | flops | bytes accessed | tf_op | source)
XLA Modules:
  0.0 42.7 jit_solution(16859009469533011820)
XLA Ops:
  0.0 42.0 %shard_map.55 = bf16[768,128]{1,0:T(8,128)(2,1)S(1)} custom-call(s32[4,6]{1,0:T(4,128)} %bitcast.7, s32[4,6]{1,0:T(4,128)} %bitcast.8, s32[4]{0:T(128)} %bitcast.9, bf16[12,512,128]{2,1,0:T(8,128)(2,1)} %bitcast.6, bf16[128,256]{1,0:T(8,128)(2,1)} %w_hbm.1), custom_call_target="tpu_custom_call" | custom-call | tf_op jit(solution)/shard_map/pallas_call | solution.py:456
  42.0 0.7 %copy.7 = bf16[1,768,128]{2,1,0:T(8,128)(2,1)} copy(bf16[1,768,128]{2,1,0:T(8,128)(2,1)S(1)} %bitcast.5) | data formatting | bytes 393216

commit v6 on v5

--- a/solution.py
+++ b/solution.py
@@ -389,6 +389,11 @@
                     acc = term if acc is None else acc + term
                 put(i, acc, True)
 
+    for j in range(per_owner):
+        rows_f32 = att[j]
+        mean_square = jnp.mean(rows_f32 * rows_f32, axis=-1, keepdims=True)
+        att[j] = rows_f32 * lax.rsqrt(mean_square + 1e-06)
+
     source_other = sources[0]
     for j in range(1, per_owner):
         source_other = jnp.where(sides[j] == 1, sources[j], source_other)
@@ -399,9 +404,7 @@
             at = jnp.int32(0)
             for j in range(per_owner):
                 at = jnp.where((ranks[j] == k) & (sides[j] == part), j, at)
-            rows_f32 = att[at, low:low + size, :]
-            mean_square = jnp.mean(rows_f32 * rows_f32, axis=-1, keepdims=True)
-            normed = rows_f32 * lax.rsqrt(mean_square + 1e-06)
+            normed = att[at, low:low + size, :]
             update = recv_u[c][side_source[part]].astype(jnp.float32)
             gated[c][my_head, part * size:(part + 1) * size, :] = (normed * update).astype(jnp.bfloat16)
         for offset in range(1, heads):

time: 42.9 us -> 42.8 us (level)
  no operation moved by 1% of the time
where the time goes in v6:
time: 42.8 us; the launch traced here: 42.6 us
  Pallas kernels  41.9 us (98%)
  local copies, waits for them, and re-layouts  0.68 us (2%)
    pallas_call x1, Pallas kernels, body(): pl.pallas_call(functools.partial(kernel, (groups, ctxs, heads, per_owner,...  41.9 us

profile of v6, /device:TPU:8, one launch (start us, length us, event | category | flops | bytes accessed | tf_op | source)
XLA Modules:
  0.0 42.6 jit_solution(11200604128628698219)
XLA Ops:
  0.0 41.9 %shard_map.55 = bf16[768,128]{1,0:T(8,128)(2,1)S(1)} custom-call(s32[4,6]{1,0:T(4,128)} %bitcast.7, s32[4,6]{1,0:T(4,128)} %bitcast.8, s32[4]{0:T(128)} %bitcast.9, bf16[12,512,128]{2,1,0:T(8,128)(2,1)} %bitcast.6, bf16[128,256]{1,0:T(8,128)(2,1)} %w_hbm.1), custom_call_target="tpu_custom_call" | custom-call | tf_op jit(solution)/shard_map/pallas_call | solution.py:459
  41.9 0.7 %copy.7 = bf16[1,768,128]{2,1,0:T(8,128)(2,1)} copy(bf16[1,768,128]{2,1,0:T(8,128)(2,1)S(1)} %bitcast.5) | data formatting | bytes 393216

commit v7 on v6

--- a/solution.py
+++ b/solution.py
@@ -13,7 +13,8 @@
 QUERY, KEY, VALUE, UPDATE = 0, 1, 2, 3
 FIRST_KINDS = (KEY, VALUE, QUERY)
 KINDS = (*FIRST_KINDS, UPDATE)
-SPLIT = 2
+SPLIT = 4
+TOGETHER = 2
 
 
 def load_pieces(rows):
@@ -410,7 +411,7 @@
         for offset in range(1, heads):
             copy = pltpu.make_async_remote_copy(
                 src_ref=gated[c].at[my_head], dst_ref=gated[c].at[my_head],
-                send_sem=h_send.at[offset - 1], recv_sem=h_recv.at[c],
+                send_sem=h_send.at[offset - 1], recv_sem=h_recv.at[c // TOGETHER],
                 device_id={"head": lax.rem(my_head + offset, heads)}, device_id_type=MESH)
             copy.start()
     for copy in w_copies:
@@ -420,9 +421,9 @@
         pltpu.make_async_copy(all_cols, all_cols, w_recv).wait()
     sent()
     for c, (k, low, size) in enumerate(chunks):
-        if heads > 1:
-            theirs = gated[c].at[pl.ds(0, heads - 1)]
-            pltpu.make_async_copy(theirs, theirs, h_recv.at[c]).wait()
+        if heads > 1 and c % TOGETHER == 0:
+            theirs = send_buf.at[0, pl.ds(0, TOGETHER * 2 * size * (heads - 1))]
+            pltpu.make_async_copy(theirs, theirs, h_recv.at[c // TOGETHER]).wait()
         acc = None
         for h in range(heads):
             term = jnp.dot(gated[c][h], w_cols[h], preferred_element_type=jnp.float32)
@@ -481,7 +482,7 @@
             pltpu.VMEM((per_owner, rows, width), bf16),
             dma((groups + spans * half,)), dma((3 + len(chunks) + 4 * spans * half,)),
             dma((2, window)), dma((2, window)),
-            dma((max(heads - 1, 1),)), dma((len(chunks),)),
+            dma((max(heads - 1, 1),)), dma((len(chunks) // TOGETHER,)),
             dma((max(heads - 1, 1),)), dma,
             dma((2,)), pltpu.SemaphoreType.REGULAR((spans,)), pltpu.SemaphoreType.REGULAR((spans,)),
         ],

time: 42.8 us -> 42.6 us (level)
  no operation moved by 1% of the time
where the time goes in v7:
time: 42.6 us; the launch traced here: 42.5 us
  Pallas kernels  41.8 us (98%)
  local copies, waits for them, and re-layouts  0.68 us (2%)
    pallas_call x1, Pallas kernels, body(): pl.pallas_call(functools.partial(kernel, (groups, ctxs, heads, per_owner,...  41.8 us

profile of v7, /device:TPU:8, one launch (start us, length us, event | category | flops | bytes accessed | tf_op | source)
XLA Modules:
  0.0 42.5 jit_solution(8167610515313122553)
XLA Ops:
  0.0 41.8 %shard_map.55 = bf16[768,128]{1,0:T(8,128)(2,1)S(1)} custom-call(s32[4,6]{1,0:T(4,128)} %bitcast.7, s32[4,6]{1,0:T(4,128)} %bitcast.8, s32[4]{0:T(128)} %bitcast.9, bf16[12,512,128]{2,1,0:T(8,128)(2,1)} %bitcast.6, bf16[128,256]{1,0:T(8,128)(2,1)} %w_hbm.1), custom_call_target="tpu_custom_call" | custom-call | tf_op jit(solution)/shard_map/pallas_call | solution.py:460
  41.8 0.7 %copy.7 = bf16[1,768,128]{2,1,0:T(8,128)(2,1)} copy(bf16[1,768,128]{2,1,0:T(8,128)(2,1)S(1)} %bitcast.5) | data formatting | bytes 393216

commit v8 on v7

--- a/solution.py
+++ b/solution.py
@@ -420,6 +420,11 @@
         all_cols = w_cols.at[pl.ds(0, heads - 1)]
         pltpu.make_async_copy(all_cols, all_cols, w_recv).wait()
     sent()
+    for offset in range(1, window + 1):
+        @pl.when(my_ctx + offset < ctxs)
+        def _():
+            ctx_copy(0, own_k, prev_k, offset).wait_send()
+            ctx_copy(1, own_v, prev_v, offset).wait_send()
     for c, (k, low, size) in enumerate(chunks):
         if heads > 1 and c % TOGETHER == 0:
             theirs = send_buf.at[0, pl.ds(0, TOGETHER * 2 * size * (heads - 1))]
@@ -437,11 +442,6 @@
             device_id={"head": my_head}, device_id_type=MESH).wait_send()
     for j in range(per_owner):
         out_ref[j * rows:(j + 1) * rows, :] = mixed[2 * ranks[j] + sides[j]]
-    for offset in range(1, window + 1):
-        @pl.when(my_ctx + offset < ctxs)
-        def _():
-            ctx_copy(0, own_k, prev_k, offset).wait_send()
-            ctx_copy(1, own_v, prev_v, offset).wait_send()
 
 
 def body(ingest, src_shard, src_slot, hist_len, w_out):

time: 42.6 us -> 42.6 us (level)
  no operation moved by 1% of the time
where the time goes in v8:
time: 42.6 us; the launch traced here: 42.5 us
  Pallas kernels  41.8 us (98%)
  local copies, waits for them, and re-layouts  0.68 us (2%)
    pallas_call x1, Pallas kernels, body(): pl.pallas_call(functools.partial(kernel, (groups, ctxs, heads, per_owner,...  41.8 us

profile of v8, /device:TPU:8, one launch (start us, length us, event | category | flops | bytes accessed | tf_op | source)
XLA Modules:
  0.0 42.5 jit_solution(13867764372487747263)
XLA Ops:
  0.0 41.8 %shard_map.55 = bf16[768,128]{1,0:T(8,128)(2,1)S(1)} custom-call(s32[4,6]{1,0:T(4,128)} %bitcast.7, s32[4,6]{1,0:T(4,128)} %bitcast.8, s32[4]{0:T(128)} %bitcast.9, bf16[12,512,128]{2,1,0:T(8,128)(2,1)} %bitcast.6, bf16[128,256]{1,0:T(8,128)(2,1)} %w_hbm.1), custom_call_target="tpu_custom_call" | custom-call | tf_op jit(solution)/shard_map/pallas_call | solution.py:460
  41.8 0.7 %copy.7 = bf16[1,768,128]{2,1,0:T(8,128)(2,1)} copy(bf16[1,768,128]{2,1,0:T(8,128)(2,1)S(1)} %bitcast.5) | data formatting | bytes 393216
